TPU v7x, 512 devices: a whole 4x4x16 slice. The times are simulated.
512 devices in a mesh: dp: 16 (over x_hi, y, core), factor: 32 (over x_lo, z).
Axes of the slice: x: 4 (x_hi: 2, x_lo: 2; x = x_hi * 2 + x_lo), y: 4, z: 16, core: 2. Of those that a mesh axis runs over, the one named last changes fastest.
Arguments:
- activations: bfloat16 [2048, 8192], P('dp', 'factor'), may hold values from -12 to 12
- gradients: bfloat16 [2048, 8192], P('dp', 'factor'), may hold values from -12 to 12
- act_basis: bfloat16 [8192, 8192], P('dp', 'factor'), may hold values from -0.0625 to 0.0625
- grad_basis: bfloat16 [8192, 8192], P('dp', 'factor'), may hold values from -0.0625 to 0.0625
Outputs:
- corrected: float32 [8192, 8192], P('factor', 'dp')
All inputs are finite; a program needn't handle non-finite values.
Results may differ from a plain program's by a relative error of at most 0.00062.
Values may be sent and summed in bfloat16 or wider, within the bound.
No kernel may reach another device: no remote copies, remote signals or barrier semaphores. Data moves between devices by JAX's collectives and lax.ppermute only.
A program may use at most 64 MiB of HBM per device.

v0:
```python
import jax
import jax.numpy as jnp
from jax import lax
from jax.sharding import PartitionSpec as P


def on_device(activations, gradients, act_basis, grad_basis):
    act_full, grad_full = (
        lax.all_gather(activations, "factor", axis=1, tiled=True),
        lax.all_gather(gradients, "factor", axis=1, tiled=True),
    )
    columns = act_full
    rotated_act = jnp.dot(
        columns,
        lax.all_gather(act_basis, "dp", axis=0, tiled=True),
        preferred_element_type=jnp.float32,
    )
    columns = grad_full
    rotated_grad = jnp.dot(
        columns,
        lax.all_gather(grad_basis, "dp", axis=0, tiled=True),
        preferred_element_type=jnp.float32,
    )
    act_square = (rotated_act * rotated_act).astype(jnp.bfloat16)
    grad_square = (rotated_grad * rotated_grad).astype(jnp.bfloat16)
    act_every = lax.all_gather(act_square, "dp", axis=0, tiled=True)
    grad_wide = lax.all_gather(grad_square, "factor", axis=1, tiled=True)
    grad_block = lax.all_to_all(grad_wide, "dp", split_axis=1, concat_axis=0, tiled=True)
    total = lax.dot_general(
        act_every, grad_block, (((0,), (0,)), ((), ())), preferred_element_type=jnp.float32
    )
    return total * (1.0 / act_every.shape[0])


def solution(mesh):
    return jax.shard_map(
        on_device,
        mesh=mesh,
        in_specs=(P("dp", "factor"), P("dp", "factor"), P("dp", "factor"), P("dp", "factor")),
        out_specs=P("factor", "dp"),
        check_vma=False,
    )
```

profile of v0, /device:TPU:1, one launch (start us, length us, event | category | flops | bytes accessed | tf_op | source)
XLA Modules:
  0.0 617.3 jit_solution(8077619885345062295)
XLA Ops:
  6.5 0.0 all-gather.13.cloned.1.call-start
  6.5 0.7 all-gather.13.cloned.1.call-update
  7.3 0.0 all-gather.15.cloned.1.call-start
  7.3 0.7 all-gather.15.cloned.1.call-update
  8.0 0.0 all-gather.7.cloned.1.call-start
  8.1 0.7 all-gather.7.cloned.1.call-update
  8.7 0.0 all-gather.9.cloned.1.call-start
  8.8 0.5 all-gather.9.cloned.1.call-update
  9.3 0.0 all-gather.17.cloned.1.call-start
  9.4 111.3 %all-gather.13.cloned.1.call-done = bf16[128,8192]{1,0:T(8,128)(2,1)} async-done(((bf16[128,256]{1,0:T(8,128)(2,1)}), bf16[128,8192]{1,0:T(8,128)(2,1)}) %all-gather.13.cloned.1.call-update) | async-done | bytes 2097168 | tf_op jit(solution)/shard_map/all_gather | solution.py:10
  120.7 92.8 %all-gather.15.cloned.1.call-done = bf16[8192,256]{1,0:T(8,128)(2,1)} async-done(((bf16[512,256]{1,0:T(8,128)(2,1)}), bf16[8192,256]{1,0:T(8,128)(2,1)}) %all-gather.15.cloned.1.call-update) | async-done | bytes 4194320 | tf_op jit(solution)/shard_map/all_gather | solution.py:21
  213.5 4.2 fusion.1
  217.6 0.0 all-gather.17.cloned.1.call-update
  217.6 0.0 all-gather.11.cloned.1.call-start
  217.7 101.3 %all-gather.7.cloned.1.call-done = bf16[128,8192]{1,0:T(8,128)(2,1)} async-done(((bf16[128,256]{1,0:T(8,128)(2,1)}), bf16[128,8192]{1,0:T(8,128)(2,1)}) %all-gather.7.cloned.1.call-update) | async-done | bytes 2097168 | tf_op jit(solution)/shard_map/all_gather | solution.py:9
  319.0 92.6 %all-gather.9.cloned.1.call-done = bf16[8192,256]{1,0:T(8,128)(2,1)} async-done(((bf16[512,256]{1,0:T(8,128)(2,1)}), bf16[8192,256]{1,0:T(8,128)(2,1)}) %all-gather.9.cloned.1.call-update) | async-done | bytes 4194320 | tf_op jit(solution)/shard_map/all_gather | solution.py:15
  411.7 4.2 fusion
  415.8 0.0 all-gather.11.cloned.1.call-update
  415.8 101.2 %all-gather.17.cloned.1.call-done = bf16[128,8192]{1,0:T(8,128)(2,1)} async-done(((bf16[128,256]{1,0:T(8,128)(2,1)}), bf16[128,8192]{1,0:T(8,128)(2,1)}) %all-gather.17.cloned.1.call-update) | async-done | bytes 2097168 | tf_op jit(solution)/shard_map/all_gather | solution.py:27
  517.1 3.2 copy.8
  520.2 29.6 %all-to-all-start = ((bf16[128,16,512]{2,0,1:T(8,128)(2,1)}), bf16[128,16,512]{2,0,1:T(8,128)(2,1)S(1)}, u32[]{:S(2)}, u32[]{:S(2)}) async-start(bf16[128,16,512]{2,0,1:T(8,128)(2,1)} %bitcast.12), calls=%async_computation | async-start | bytes 4194304 | tf_op jit(solution)/shard_map/all_to_all | solution.py:28
  549.8 57.8 %all-gather.11.cloned.1.call-done = bf16[2048,256]{1,0:T(8,128)(2,1)} async-done(((bf16[128,256]{1,0:T(8,128)(2,1)}), bf16[2048,256]{1,0:T(8,128)(2,1)}) %all-gather.11.cloned.1.call-update) | async-done | bytes 1048592 | tf_op jit(solution)/shard_map/all_gather | solution.py:26
  607.7 0.0 all-to-all-done
  607.7 2.7 convolution_multiply_fusion
Async XLA Ops:
  6.5 114.2 %all-gather.13.cloned.1.call-start = ((), (), s32[]{:S(2)}) async-start(), calls=%async_computation.4 | async-start | bytes 2162688 | tf_op jit(solution)/shard_map/all_gather | solution.py:10
  7.3 206.2 %all-gather.15.cloned.1.call-start = ((), (), s32[]{:S(2)}) async-start(), calls=%async_computation.5 | async-start | bytes 4456448 | tf_op jit(solution)/shard_map/all_gather | solution.py:21
  8.0 311.0 %all-gather.7.cloned.1.call-start = ((), (), s32[]{:S(2)}) async-start(), calls=%async_computation.1 | async-start | bytes 2162688 | tf_op jit(solution)/shard_map/all_gather | solution.py:9
  8.7 402.9 %all-gather.9.cloned.1.call-start = ((), (), s32[]{:S(2)}) async-start(), calls=%async_computation.2 | async-start | bytes 4456448 | tf_op jit(solution)/shard_map/all_gather | solution.py:15
  9.3 507.7 %all-gather.17.cloned.1.call-start = ((), (), s32[]{:S(2)}) async-start(), calls=%async_computation.6 | async-start | bytes 2162688 | tf_op jit(solution)/shard_map/all_gather | solution.py:27
  217.6 390.0 %all-gather.11.cloned.1.call-start = ((), (), s32[]{:S(2)}) async-start(), calls=%async_computation.3 | async-start | bytes 1114112 | tf_op jit(solution)/shard_map/all_gather | solution.py:26
  520.2 87.5 %all-to-all-start = ((bf16[128,16,512]{2,0,1:T(8,128)(2,1)}), bf16[128,16,512]{2,0,1:T(8,128)(2,1)S(1)}, u32[]{:S(2)}, u32[]{:S(2)}) async-start(bf16[128,16,512]{2,0,1:T(8,128)(2,1)} %bitcast.12), calls=%async_computation | async-start | bytes 4194304 | tf_op jit(solution)/shard_map/all_to_all | solution.py:28
Sparse Core Ops, SparseCore 0:
  9.4 111.2 all-gather.12
  124.0 89.3 all-gather.14
  215.5 103.5 all-gather.6
  322.2 89.3 all-gather.8
  413.5 103.5 all-gather.16
  520.3 87.3 all-gather.10
where the time goes:
time: 617 us
  waiting for transfers between devices  560 us (91%)
  starting transfers between devices  29.8 us (5%)
  between operations  13.5 us (2%)
  matrix products  11.1 us (2%)
    all_gather x1, waiting for transfers between devices, on_device(): lax.all_gather(gradients, 'factor', axis=1, tiled=True)  111 us
    all_gather x1, waiting for transfers between devices, on_device(): lax.all_gather(activations, 'factor', axis=1, tiled=True)  101 us
    all_gather x1, waiting for transfers between devices, on_device(): grad_wide = lax.all_gather(grad_square, 'factor', axis=1, tiled=True)  101 us
    all_gather x1, waiting for transfers between devices, on_device(): lax.all_gather(grad_basis, 'dp', axis=0, tiled=True)  92.8 us
    all_gather x1, waiting for transfers between devices, on_device(): lax.all_gather(act_basis, 'dp', axis=0, tiled=True)  92.6 us
    all_gather x1, waiting for transfers between devices, on_device(): act_every = lax.all_gather(act_square, 'dp', axis=0, tiled=True)  57.8 us
    all_to_all x1, starting transfers between devices, on_device(): lax.all_to_all(grad_wide, 'dp', split_axis=1, concat_axis=0, tiled=True)  29.6 us
  transfers between devices with their start and end apart: 7, of which 6 were waited for; matrix products, arithmetic and copies ran while one was open for 2% of the time, Pallas kernels for 0%

commit v1 on v0

--- a/solution.py
+++ b/solution.py
@@ -23,7 +23,9 @@
     )
     act_square = (rotated_act * rotated_act).astype(jnp.bfloat16)
     grad_square = (rotated_grad * rotated_grad).astype(jnp.bfloat16)
-    act_every = lax.all_gather(act_square, "dp", axis=0, tiled=True)
+    act_every = jnp.concatenate(
+        lax.all_to_all(jnp.stack([act_square] * lax.axis_size("dp")), "dp", 0, 0), axis=0
+    )
     grad_wide = lax.all_gather(grad_square, "factor", axis=1, tiled=True)
     grad_block = lax.all_to_all(grad_wide, "dp", split_axis=1, concat_axis=0, tiled=True)
     total = lax.dot_general(

time: 617 us -> 585 us (0.948)
  waiting for transfers between devices: 560 us -> 497 us
  blocking collectives: 0 us -> 57 us
  starting transfers between devices: 29.8 us -> 3.84 us
    all_gather x1 -> x0, waiting for transfers between devices: 57.8 us -> none  [on_device(): act_every = lax.all_gather(act_square, 'dp', axis=0, tiled=True)]
    all_to_all x0 -> x1, blocking collectives: none -> 57 us  [on_device(): lax.all_to_all(grad_wide, 'dp', split_axis=1, concat_axis=0, tiled=True)]
    all_to_all x1, starting transfers between devices: 29.6 us -> 3.69 us  [on_device(): lax.all_to_all(jnp.stack([act_square] * lax.axis_size('dp')), 'dp', 0, 0)]
  transfers between devices with their start and end apart: 7 -> 6, of which waited for: 6 -> 5; matrix products, arithmetic and copies ran while one was open for 2% -> 2% of each run, Pallas kernels for 0% -> 0%
where the time goes in v1:
time: 585 us; the launch traced here: 584 us
  waiting for transfers between devices  497 us (85%)
  blocking collectives  57 us (10%)
  between operations  13.2 us (2%)
  matrix products  10.2 us (2%)
    all_gather x1, waiting for transfers between devices, on_device(): lax.all_gather(gradients, 'factor', axis=1, tiled=True)  111 us
    all_gather x1, waiting for transfers between devices, on_device(): lax.all_gather(activations, 'factor', axis=1, tiled=True)  101 us
    all_gather x1, waiting for transfers between devices, on_device(): grad_wide = lax.all_gather(grad_square, 'factor', axis=1, tiled=True)  96.5 us
    all_gather x1, waiting for transfers between devices, on_device(): lax.all_gather(grad_basis, 'dp', axis=0, tiled=True)  92.8 us
    all_gather x1, waiting for transfers between devices, on_device(): lax.all_gather(act_basis, 'dp', axis=0, tiled=True)  92.6 us
    all_to_all x1, blocking collectives, on_device(): lax.all_to_all(grad_wide, 'dp', split_axis=1, concat_axis=0, tiled=True)  57 us
  transfers between devices with their start and end apart: 6, of which 5 were waited for; matrix products, arithmetic and copies ran while one was open for 2% of the time, Pallas kernels for 0%

profile of v1, /device:TPU:1, one launch (start us, length us, event | category | flops | bytes accessed | tf_op | source)
XLA Modules:
  0.0 584.4 jit_solution(3107935663304719954)
XLA Ops:
  6.5 0.0 all-gather.10.cloned.1.call-start
  6.5 0.7 all-gather.10.cloned.1.call-update
  7.3 0.0 all-gather.12.cloned.1.call-start
  7.3 0.7 all-gather.12.cloned.1.call-update
  8.0 0.0 all-gather.6.cloned.1.call-start
  8.1 0.7 all-gather.6.cloned.1.call-update
  8.7 0.0 all-gather.8.cloned.1.call-start
  8.8 0.5 all-gather.8.cloned.1.call-update
  9.3 0.0 all-gather.14.cloned.1.call-start
  9.4 111.3 %all-gather.10.cloned.1.call-done = bf16[128,8192]{1,0:T(8,128)(2,1)} async-done(((bf16[128,256]{1,0:T(8,128)(2,1)}), bf16[128,8192]{1,0:T(8,128)(2,1)}) %all-gather.10.cloned.1.call-update) | async-done | bytes 2097168 | tf_op jit(solution)/shard_map/all_gather | solution.py:10
  120.7 92.8 %all-gather.12.cloned.1.call-done = bf16[8192,256]{1,0:T(8,128)(2,1)} async-done(((bf16[512,256]{1,0:T(8,128)(2,1)}), bf16[8192,256]{1,0:T(8,128)(2,1)}) %all-gather.12.cloned.1.call-update) | async-done | bytes 4194320 | tf_op jit(solution)/shard_map/all_gather | solution.py:21
  213.5 4.2 fusion.9
  217.6 0.0 all-gather.14.cloned.1.call-update
  217.7 101.4 %all-gather.6.cloned.1.call-done = bf16[128,8192]{1,0:T(8,128)(2,1)} async-done(((bf16[128,256]{1,0:T(8,128)(2,1)}), bf16[128,8192]{1,0:T(8,128)(2,1)}) %all-gather.6.cloned.1.call-update) | async-done | bytes 2097168 | tf_op jit(solution)/shard_map/all_gather | solution.py:9
  319.0 92.6 %all-gather.8.cloned.1.call-done = bf16[8192,256]{1,0:T(8,128)(2,1)} async-done(((bf16[512,256]{1,0:T(8,128)(2,1)}), bf16[8192,256]{1,0:T(8,128)(2,1)}) %all-gather.8.cloned.1.call-update) | async-done | bytes 4194320 | tf_op jit(solution)/shard_map/all_gather | solution.py:15
  411.7 4.6 fusion.8
  416.2 1.2 stack.2
  417.4 3.7 all-to-all-start
  421.1 96.5 %all-gather.14.cloned.1.call-done = bf16[128,8192]{1,0:T(8,128)(2,1)} async-done(((bf16[128,256]{1,0:T(8,128)(2,1)}), bf16[128,8192]{1,0:T(8,128)(2,1)}) %all-gather.14.cloned.1.call-update) | async-done | bytes 2097168 | tf_op jit(solution)/shard_map/all_gather | solution.py:29
  517.6 1.8 copy.8
  519.4 0.0 all-to-all-done
  519.4 57.0 %all_to_all.21 = bf16[128,16,512]{2,0,1:T(8,128)(2,1)S(1)} all-to-all(bf16[128,16,512]{2,0,1:T(8,128)(2,1)S(1)} %bitcast.20), channel_id=1, replica_groups=mesh['dp'=16,'factor'=32] {'dp'}, dimensions={1} | all-to-all | bytes 4194304 | tf_op jit(solution)/shard_map/all_to_all | solution.py:30
  576.3 1.5 fusion.5
Async XLA Ops:
  6.5 114.2 %all-gather.10.cloned.1.call-start = ((), (), s32[]{:S(2)}) async-start(), calls=%async_computation.4 | async-start | bytes 2162688 | tf_op jit(solution)/shard_map/all_gather | solution.py:10
  7.3 206.2 %all-gather.12.cloned.1.call-start = ((), (), s32[]{:S(2)}) async-start(), calls=%async_computation.5 | async-start | bytes 4456448 | tf_op jit(solution)/shard_map/all_gather | solution.py:21
  8.0 311.0 %all-gather.6.cloned.1.call-start = ((), (), s32[]{:S(2)}) async-start(), calls=%async_computation.2 | async-start | bytes 2162688 | tf_op jit(solution)/shard_map/all_gather | solution.py:9
  8.7 402.9 %all-gather.8.cloned.1.call-start = ((), (), s32[]{:S(2)}) async-start(), calls=%async_computation.3 | async-start | bytes 4456448 | tf_op jit(solution)/shard_map/all_gather | solution.py:15
  9.3 508.2 %all-gather.14.cloned.1.call-start = ((), (), s32[]{:S(2)}) async-start(), calls=%async_computation.6 | async-start | bytes 2162688 | tf_op jit(solution)/shard_map/all_gather | solution.py:29
  417.4 102.0 %all-to-all-start = ((bf16[16,128,256]{1,2,0:T(8,128)(2,1)}), bf16[16,128,256]{1,2,0:T(8,128)(2,1)S(1)}, u32[]{:S(2)}, u32[]{:S(2)}) async-start(bf16[16,128,256]{1,2,0:T(8,128)(2,1)} %stack.2), calls=%async_computation | async-start | bytes 2097152 | tf_op jit(solution)/shard_map/all_to_all | solution.py:27
Sparse Core Ops, SparseCore 0:
  9.4 111.2 all-gather.9
  124.0 89.3 all-gather.11
  215.5 103.5 all-gather.5
  322.2 89.3 all-gather.7
  413.5 104.0 all-gather.13
